TPU v7x, 128 devices: a whole 4x4x4 slice. The times are simulated.
128 devices in a mesh: dp: 4 (over x), seq: 32 (over z, y, core).
Axes of the slice: x: 4, y: 4, z: 4, core: 2. Of those that a mesh axis runs over, the one named last changes fastest.
Arguments:
- inputs: bfloat16 [16384, 6144], P('seq'), may hold values from -6 to 6
- qkv_weight: bfloat16 [6144, 12288], P(None, ('dp', 'seq')), may hold values from -0.078125 to 0.078125
- log_decay: float32 [32, 16384], P('dp', 'seq'), may hold values from -1 to 0, as said below
- out_gain: float32 [32, 128], P('dp'), may hold values from 0.1 to 1.9
Outputs:
- attended: bfloat16 [16384, 4096], P('seq', 'dp')
Inputs may be any that keep to these rules, and one draw needn't show every extreme that they name: `log_decay`: log of a decay factor, negative at every position.
All inputs are finite; a program needn't handle non-finite values.
Results may differ from a plain program's by a relative error of at most 0.0055.
Values may be sent and summed in bfloat16 or wider, within the bound.
No kernel may reach another device: no remote copies, remote signals or barrier semaphores. Data moves between devices by JAX's collectives and lax.ppermute only.
A program may use at most 128 MiB of HBM per device.

v0:
```python
import jax
import jax.numpy as jnp
from jax import lax
from jax.sharding import PartitionSpec as P


def prefix_2(value, axis, join, neutral):
    count, mine = (lax.axis_size(axis), lax.axis_index(axis))
    pieces = jax.tree.map(lambda part: lax.all_gather(part, axis), value)
    subtotal = jax.tree.map(
        lambda part, zero: jnp.full_like(part, 0) + jnp.asarray(zero, part.dtype), value, neutral
    )

    def turn(position, subtotal):
        longer = join(subtotal, jax.tree.map(lambda part: part[position], pieces))
        return jax.tree.map(lambda new, old: jnp.where(position < mine, new, old), longer, subtotal)

    return lax.fori_loop(0, count - 1, turn, subtotal)


def block_terms(queries, keys, values, block_decay):
    cumulated = jnp.cumsum(block_decay, axis=-1)
    tok_count = queries.shape[-2]
    row_index = jnp.arange(tok_count)[:, None]
    col_index = jnp.arange(tok_count)[None, :]
    causal = row_index >= col_index
    spread = cumulated[:, :, None] - cumulated[:, None, :]
    decay_mask = jnp.where(causal, jnp.exp(jnp.where(causal, spread, 0.0)), 0.0)
    scores = jnp.einsum("htd,hsd->hts", queries, keys, preferred_element_type=jnp.float32)
    weights = (scores * decay_mask).astype(jnp.bfloat16)
    intra_term = jnp.einsum("hts,hsd->htd", weights, values, preferred_element_type=jnp.float32)
    tail_decay = jnp.exp(cumulated[:, -1:] - cumulated)
    keys_decayed = keys.astype(jnp.float32) * tail_decay[:, :, None]
    update = jnp.einsum(
        "hsd,hse->hde", keys_decayed, values.astype(jnp.float32), precision=lax.Precision.HIGHEST
    )
    block_total = cumulated[:, -1]
    queries_decayed = queries.astype(jnp.float32) * jnp.exp(cumulated)[:, :, None]
    return (intra_term, update, block_total, queries_decayed)


def finish_heads(intra_term, queries_decayed, carried, gains):
    outer_term = jnp.einsum(
        "htd,hde->hte", queries_decayed, carried, precision=lax.Precision.HIGHEST
    )
    combined = intra_term + outer_term
    root_mean = lax.rsqrt(jnp.mean(combined * combined, axis=-1, keepdims=True) + 1e-05)
    return combined * root_mean * gains[:, None, :]


def chain_combine(earlier_pair, later_pair):
    return (
        earlier_pair[0] + later_pair[0],
        jnp.exp(later_pair[0])[:, None, None] * earlier_pair[1] + later_pair[1],
    )


def shards(inputs, qkv_weight, log_decay, out_gain):
    tok_count = inputs.shape[0]
    local_heads = out_gain.shape[0]
    head_size = out_gain.shape[1]
    projected = jnp.dot(
        inputs,
        lax.all_gather(qkv_weight, "seq", axis=1, tiled=True),
        preferred_element_type=jnp.float32,
    )
    activated = jax.nn.silu(projected).astype(jnp.bfloat16)
    grouped = jnp.transpose(activated.reshape(tok_count, local_heads, 3, head_size), (2, 1, 0, 3))
    intra_term, update, block_total, queries_decayed = block_terms(
        grouped[0], grouped[1], grouped[2], log_decay
    )
    identity = (jnp.zeros_like(block_total), jnp.zeros_like(update))
    prefix = prefix_2((block_total, update), "seq", chain_combine, identity)
    normed = finish_heads(intra_term, queries_decayed, prefix[1], out_gain)
    return (
        jnp.transpose(normed, (1, 0, 2))
        .reshape(tok_count, local_heads * head_size)
        .astype(jnp.bfloat16)
    )


def solution(mesh):
    in_specs = (P("seq", None), P(None, ("dp", "seq")), P("dp", "seq"), P("dp", None))
    out_specs = P("seq", "dp")
    return jax.shard_map(shards, mesh=mesh, in_specs=in_specs, out_specs=out_specs, check_vma=False)
```

profile of v0, /device:TPU:0, one launch (start us, length us, event | category | flops | bytes accessed | tf_op | source)
XLA Modules:
  0.0 301.2 jit_solution(9660974679958368231)
XLA Ops:
  6.5 0.7 all-gather.5.cloned.1.call-update
  7.3 2.2 reduce-window.6
  9.5 0.2 slice_reduce_fusion
  9.8 0.2 slice_reduce_fusion.1
  10.1 126.8 %all-gather.5.cloned.1.call-done = bf16[6144,3072]{0,1:T(8,128)(2,1)} async-done(((bf16[6144,96]{0,1:T(8,128)(2,1)}), bf16[6144,3072]{0,1:T(8,128)(2,1)}) %all-gather.5.cloned.1.call-update) | async-done | bytes 37748752 | tf_op jit(solution)/shard_map/all_gather | solution.py:64
  136.8 28.2 %multiply_convert_fusion.1 = bf16[512,3072]{1,0:T(8,128)(2,1)} fusion(bf16[512,6144]{1,0:T(8,128)(2,1)} %param.6, bf16[6144,3072]{0,1:T(8,128)(2,1)} %all-gather.5.cloned.1.call-done), kind=kOutput, calls=%fused_computation.4 | convolution fusion | flops 19335217152 | bytes 47185920 | tf_op jit(solution)/shard_map/dot_general | solution.py:62
  165.0 3.2 %copy.26 = bf16[512,3072]{0,1:T(8,128)(2,1)S(1)} copy(bf16[512,3072]{1,0:T(8,128)(2,1)} %multiply_convert_fusion.1) | data formatting | bytes 6291456 | tf_op jit(solution)/shard_map/convert_element_type | solution.py:67
  168.2 2.8 copy.27
  171.1 4.8 %fusion.7 = f32[8,128,128]{2,1,0:T(8,128)} fusion(f32[8,512]{1,0:T(8,128)S(1)} %subtract_exponential_fusion, bf16[3,8,512,128]{3,2,1,0:T(8,128)(2,1)} %bitcast.51), kind=kOutput, calls=%fused_computation.12 | convolution fusion | flops 806354944 | bytes 2637824 | tf_op jit(solution)/shard_map/hsd,hse->hde/dot_general | solution.py:34
  175.9 0.6 dynamic-slice
  177.1 0.2 dynamic-update-slice
  177.3 67.5 %all-reduce = f32[256]{0:T(256)S(1)} all-reduce(f32[256]{0:T(256)S(1)} %dynamic-update-slice), channel_id=2, replica_groups=mesh['dp'=4,'seq'=32] {'seq'}, use_global_device_ids=true, to_apply=%add | all-reduce | flops 256 | bytes 2048
  245.0 5.7 %fusion.1 = f32[8,512,128]{1,2,0:T(8,128)S(1)} fusion(f32[8,512]{1,0:T(8,128)S(1)} %get-tuple-element.129, pred[512,512]{1,0:T(8,128)(4,1)S(1)} %iota_compare_fusion, bf16[3,8,512,128]{3,2,1,0:T(8,128)(2,1)} %bitcast.52), kind=kOutput, calls=%fused_computation.5 | convolution fusion | flops 1084227584 | bytes 5537792 | tf_op jit(solution)/shard_map/hts,hsd->htd/dot_general | solution.py:31
  250.8 37.9 %while.14 = (s32[]{:T(128)}, f32[8,128,128]{2,1,0:T(8,128)S(1)}, s32[]{:T(128)}, f32[32,8]{1,0:T(8,128)S(1)}, f32[32,8,128,128]{3,2,1,0:T(8,128)}, /*index=5*/s32[]{:T(128)}, s32[]{:T(128)}) while((s32[]{:T(128)}, f32[8,128,128]{2,1,0:T(8,128)S(1)}, s32[]{:T(128)}, f32[32,8]{1,0:T(8,128)S(1)}, f32[32,8,128,128]{3,2,1,0:T(8,128)}, ...), condition=%wide.region_3.4_spmd.clone, body=%wide.region_2.3_spmd.clone.sunk | while | flops 524292 | bytes 1573073 | solution.py:18
  250.8 1.2 fusion.24
  252.0 1.2 fusion.24
  253.3 1.2 fusion.24
  254.5 1.2 fusion.24
  255.7 1.2 fusion.24
  256.9 1.2 fusion.24
  258.2 1.2 fusion.24
  259.4 1.2 fusion.24
  260.6 1.2 fusion.24
  261.8 1.2 fusion.24
  263.1 1.2 fusion.24
  264.3 1.2 fusion.24
  265.5 1.2 fusion.24
  266.7 1.2 fusion.24
  268.0 1.2 fusion.24
  269.2 1.2 fusion.24
  270.4 1.2 fusion.24
  271.6 1.2 fusion.24
  272.9 1.2 fusion.24
  274.1 1.2 fusion.24
  275.3 1.2 fusion.24
  276.5 1.2 fusion.24
  277.7 1.2 fusion.24
  279.0 1.2 fusion.24
  280.2 1.2 fusion.24
  281.4 1.2 fusion.24
  282.6 1.2 fusion.24
  283.9 1.2 fusion.24
  285.1 1.2 fusion.24
  286.3 1.2 fusion.24
  287.5 1.2 fusion.24
  288.7 4.0 %multiply_reduce_fusion = (f32[8,512]{1,0:T(8,128)S(1)}, f32[8,512,128]{1,2,0:T(8,128)S(1)}) fusion(f32[8,512,128]{1,2,0:T(8,128)S(1)} %fusion.1, f32[8,128,128]{2,1,0:T(8,128)S(1)} %get-tuple-element.99, f32[8,512]{1,0:T(8,128)S(1)} %get-tuple-element.128, bf16[3,8,512,128]{3,2,1,0:T(8,128)(2,1)} %bitcast.53), kind=kOutput, calls=%fused_computation.11 | convolution fusion | flops 807923712 | bytes 5799936 | tf_op jit(solution)/shard_map/htd,hde->hte/dot_general | solution.py:43
  292.7 0.3 fusion.6
  293.1 1.3 copy.31
  (48 shorter events, 0.9 us)
Async XLA Ops:
  6.5 130.3 %all-gather.5.cloned.1.call-start = ((), (), s32[]{:S(2)}) async-start(), calls=%async_computation | async-start | bytes 38928384 | tf_op jit(solution)/shard_map/all_gather | solution.py:64
  7.3 243.5 %all-gather.7.cloned.1.call-start = ((), (), s32[]{:S(2)}) async-start(), calls=%async_computation.1 | async-start | bytes 17301504 | tf_op jit(solution)/shard_map/all_gather | solution.py:9
  171.1 4.8 %copy-start.1 = (u32[128]{0:T(128)S(1)}, u32[128]{0:T(128)}, u32[]{:S(2)}) copy-start(u32[128]{0:T(128)} %constant.45) | copy-start | bytes 1540
  288.7 4.0 %copy-start = (f32[8,128]{1,0:T(8,128)S(1)}, f32[8,128]{1,0:T(8,128)}, u32[]{:S(2)}) copy-start(f32[8,128]{1,0:T(8,128)} %param.9) | copy-start | bytes 12292
Sparse Core Ops, SparseCore 0:
  9.6 127.2 all-gather.4
  176.0 72.2 all-gather.6
where the time goes:
time: 303 us; the launch traced here: 301 us
  waiting for transfers between devices  128 us (42%)
  blocking collectives  67.5 us (22%)
  matrix products  42.6 us (14%)
  other arithmetic  39.3 us (13%)
  between operations  14.1 us (5%)
  local copies, waits for them, and re-layouts  9.05 us (3%)
    all_gather x1, waiting for transfers between devices, shards(): lax.all_gather(qkv_weight, 'seq', axis=1, tiled=True)  127 us
    unnamed x1, blocking collectives  67.5 us
    select_n x31, other arithmetic, turn(): jnp.where(position < mine, new, old)  36.5 us
    dot_general x1, matrix products, shards(): jnp.dot(inputs, lax.all_gather(qkv_weight, 'seq', axis=1, tiled=True), pr...  28.2 us
  transfers between devices with their start and end apart: 2, of which 1 were waited for; matrix products, arithmetic and copies ran while one was open for 3% of the time, Pallas kernels for 0%

commit v1 on v0

--- a/solution.py
+++ b/solution.py
@@ -56,14 +56,19 @@
 
 
 def shards(inputs, qkv_weight, log_decay, out_gain):
+
+    def joints_build(chip_axis, field_in):
+        return jnp.concatenate(
+            lax.all_to_all(
+                jnp.stack([field_in] * lax.axis_size(chip_axis), axis=0), chip_axis, 0, 0
+            ),
+            1,
+        )
+
     tok_count = inputs.shape[0]
     local_heads = out_gain.shape[0]
     head_size = out_gain.shape[1]
-    projected = jnp.dot(
-        inputs,
-        lax.all_gather(qkv_weight, "seq", axis=1, tiled=True),
-        preferred_element_type=jnp.float32,
-    )
+    projected = jnp.dot(inputs, joints_build("seq", qkv_weight), preferred_element_type=jnp.float32)
     activated = jax.nn.silu(projected).astype(jnp.bfloat16)
     grouped = jnp.transpose(activated.reshape(tok_count, local_heads, 3, head_size), (2, 1, 0, 3))
     intra_term, update, block_total, queries_decayed = block_terms(

time: 303 us -> 686 us (2.26)
  waiting for transfers between devices: 128 us -> 492 us
  local copies, waits for them, and re-layouts: 9.05 us -> 22.2 us
  starting transfers between devices: 0.04 us -> 8.74 us
    all_to_all x0 -> x1, waiting for transfers between devices: none -> 491 us  [joints_build(): lax.all_to_all(jnp.stack([field_in] * lax.axis_size(chip_axis), axis=0),...]
    all_gather x1 -> x0, waiting for transfers between devices: 127 us -> none  [shards(): lax.all_gather(qkv_weight, 'seq', axis=1, tiled=True)]
    another operation x1 -> x2, local copies, waits for them, and re-layouts: 0.01 us -> 13.2 us  [the longest x1 13.2 us: joints_build(): jnp.stack([field_in] * lax.axis_size(chip_axis), axis=0)]
    all_to_all x0 -> x1, starting transfers between devices: none -> 8.7 us  [joints_build(): lax.all_to_all(jnp.stack([field_in] * lax.axis_size(chip_axis), axis=0),...]
  transfers between devices with their start and end apart: 2 -> 2, of which waited for: 1 -> 1; matrix products, arithmetic and copies ran while one was open for 3% -> 1% of each run, Pallas kernels for 0% -> 0%
where the time goes in v1:
time: 686 us; the launch traced here: 684 us
  waiting for transfers between devices  492 us (72%)
  blocking collectives  65.3 us (10%)
  matrix products  42.7 us (6%)
  other arithmetic  38.1 us (6%)
  local copies, waits for them, and re-layouts  22.2 us (3%)
  between operations  14.2 us (2%)
  starting transfers between devices  8.74 us (1%)
    all_to_all x1, waiting for transfers between devices, joints_build(): lax.all_to_all(jnp.stack([field_in] * lax.axis_size(chip_axis), axis=0),...  491 us
    unnamed x1, blocking collectives  65.3 us
    select_n x31, other arithmetic, turn(): jnp.where(position < mine, new, old)  36.4 us
    dot_general x1, matrix products, shards(): jnp.dot(inputs, joints_build('seq', qkv_weight), preferred_element_type=j...  28.2 us
  transfers between devices with their start and end apart: 2, of which 1 were waited for; matrix products, arithmetic and copies ran while one was open for 1% of the time, Pallas kernels for 0%

profile of v1, /device:TPU:0, one launch (start us, length us, event | category | flops | bytes accessed | tf_op | source)
XLA Modules:
  0.0 683.6 jit_solution(14940728624341877715)
XLA Ops:
  6.5 13.2 %stack.2 = bf16[32,6144,96]{1,2,0:T(8,128)(2,1)} broadcast(bf16[6144,96]{0,1:T(8,128)(2,1)} %param.7), dimensions={1,2} | broadcast | bytes 38928384 | tf_op jit(solution)/shard_map/stack | solution.py:63
  19.7 8.7 %all-to-all-start = ((bf16[32,6144,96]{1,2,0:T(8,128)(2,1)}), bf16[32,6144,96]{1,2,0:T(8,128)(2,1)}, u32[]{:S(2)}, u32[]{:S(2)}) async-start(bf16[32,6144,96]{1,2,0:T(8,128)(2,1)} %stack.2), calls=%async_computation | async-start | bytes 75497472 | tf_op jit(solution)/shard_map/all_to_all | solution.py:62
  28.5 1.1 reduce-window.6
  29.9 0.2 slice_reduce_fusion.1
  30.2 491.5 %all-to-all-done = bf16[32,6144,96]{1,2,0:T(8,128)(2,1)} async-done(((bf16[32,6144,96]{1,2,0:T(8,128)(2,1)}), bf16[32,6144,96]{1,2,0:T(8,128)(2,1)}, u32[]{:S(2)}, u32[]{:S(2)}) %all-to-all-start) | async-done | bytes 37748768 | tf_op jit(solution)/shard_map/all_to_all | solution.py:62
  521.6 28.2 %multiply_convert_fusion.1 = bf16[512,3072]{1,0:T(8,128)(2,1)} fusion(bf16[512,6144]{1,0:T(8,128)(2,1)} %param.6, bf16[6144,3072]{0,1:T(8,128)(2,1)} %bitcast.1), kind=kOutput, calls=%fused_computation.4 | convolution fusion | flops 19335217152 | bytes 47185920 | tf_op jit(solution)/shard_map/dot_general | solution.py:71
  549.9 3.2 copy.27
  553.0 2.8 copy.28
  555.9 4.8 fusion.7
  560.7 0.6 dynamic-slice
  562.0 0.2 dynamic-update-slice
  562.2 65.3 %all-reduce = f32[256]{0:T(256)S(1)} all-reduce(f32[256]{0:T(256)S(1)} %dynamic-update-slice), channel_id=2, replica_groups=mesh['dp'=4,'seq'=32] {'seq'}, use_global_device_ids=true, to_apply=%add | all-reduce | flops 256 | bytes 2048
  627.7 5.7 fusion.1
  633.4 37.7 %while.14 = (s32[]{:T(128)}, f32[8,128,128]{2,1,0:T(8,128)S(1)}, s32[]{:T(128)}, f32[32,8]{1,0:T(8,128)S(1)}, f32[32,8,128,128]{3,2,1,0:T(8,128)}, /*index=5*/s32[]{:T(128)}, s32[]{:T(128)}) while((s32[]{:T(128)}, f32[8,128,128]{2,1,0:T(8,128)S(1)}, s32[]{:T(128)}, f32[32,8]{1,0:T(8,128)S(1)}, f32[32,8,128,128]{3,2,1,0:T(8,128)}, ...), condition=%wide.region_3.4_spmd.clone, body=%wide.region_2.3_spmd.clone.sunk | while | flops 524292 | bytes 1573065 | solution.py:18
  633.4 1.2 fusion.24
  634.7 1.2 fusion.24
  635.9 1.2 fusion.24
  637.1 1.2 fusion.24
  638.3 1.2 fusion.24
  639.5 1.2 fusion.24
  640.7 1.2 fusion.24
  641.9 1.2 fusion.24
  643.2 1.2 fusion.24
  644.4 1.2 fusion.24
  645.6 1.2 fusion.24
  646.8 1.2 fusion.24
  648.0 1.2 fusion.24
  649.2 1.2 fusion.24
  650.5 1.2 fusion.24
  651.7 1.2 fusion.24
  652.9 1.2 fusion.24
  654.1 1.2 fusion.24
  655.3 1.2 fusion.24
  656.5 1.2 fusion.24
  657.8 1.2 fusion.24
  659.0 1.2 fusion.24
  660.2 1.2 fusion.24
  661.4 1.2 fusion.24
  662.6 1.2 fusion.24
  663.8 1.2 fusion.24
  665.0 1.2 fusion.24
  666.3 1.2 fusion.24
  667.5 1.2 fusion.24
  668.7 1.2 fusion.24
  669.9 1.2 fusion.24
  671.1 4.0 multiply_reduce_fusion
  675.1 0.3 fusion.6
  675.4 1.3 copy.32
  (50 shorter events, 1.0 us)
Async XLA Ops:
  19.7 8.8 %copy-start = (f32[8,512]{1,0:T(8,128)S(1)}, f32[8,512]{1,0:T(8,128)}, u32[]{:S(2)}) copy-start(f32[8,512]{1,0:T(8,128)} %param.8) | copy-start | bytes 49156
  19.7 501.9 %all-to-all-start = ((bf16[32,6144,96]{1,2,0:T(8,128)(2,1)}), bf16[32,6144,96]{1,2,0:T(8,128)(2,1)}, u32[]{:S(2)}, u32[]{:S(2)}) async-start(bf16[32,6144,96]{1,2,0:T(8,128)(2,1)} %stack.2), calls=%async_computation | async-start | bytes 75497472 | tf_op jit(solution)/shard_map/all_to_all | solution.py:62
  28.4 605.0 %all-gather.4.cloned.1.call-start = ((), (), s32[]{:S(2)}) async-start(), calls=%async_computation.1 | async-start | bytes 17301504 | tf_op jit(solution)/shard_map/all_gather | solution.py:9
  555.9 4.8 copy-start.2
  671.1 4.0 copy-start.1
Sparse Core Ops, SparseCore 0:
  560.8 69.9 all-gather.3
